TPU v7x, 32 devices: a whole 2x2x4 slice. The times are simulated.
32 devices in a mesh: seq: 32 (over z, y, x, core), head: 1.
Axes of the slice: x: 2, y: 2, z: 4, core: 2. Of those that a mesh axis runs over, the one named last changes fastest.
Arguments:
- video_query: bfloat16 [65536, 2048], P('seq', 'head'), may hold values from -360 to 360
- video_kv: bfloat16 [2, 65536, 2048], P(None, 'seq', 'head'), may hold values from -360 to 360
- video_clip: int32 [65536], P('seq'), may hold values from 0 to 7, never falling along the last dimension, each value on 1 to 49152 neighbouring positions
- audio_hidden: bfloat16 [256, 2048], replicated, may hold values from -6 to 6
- audio_qkv_weight: bfloat16 [32, 128, 3072], P('seq', None, 'head'), may hold values from -0.125 to 0.125
- audio_clip: int32 [256], replicated, may hold values from 0 to 7, never falling along the last dimension, each value on 1 to 192 neighbouring positions
- audio_out_weight: bfloat16 [2048, 2048], P('head', 'seq'), may hold values from -0.125 to 0.125
Outputs:
- video_attn: bfloat16 [65536, 2048], P('seq', 'head')
- audio_out: bfloat16 [256, 2048], P('head', 'seq')
Inputs may be any that keep to these rules, and one draw needn't show every extreme that they name: `video_clip`: rows of one clip are consecutive; every clip number appears among the video rows. `audio_clip`: rows of one clip are consecutive; every clip number appears among the audio rows.
All inputs are finite; a program needn't handle non-finite values.
Results may differ from a plain program's by a relative error of at most 0.009.
The roundings to bfloat16 on the way count: a program that leaves them out, or rounds other values in their place, can miss the bound.
Values may be sent and summed in bfloat16 or wider, within the bound.
No kernel may reach another device: no remote copies, remote signals or barrier semaphores. Data moves between devices by JAX's collectives and lax.ppermute only.
A program may use at most 128 MiB of HBM per device.

v0:
```python
import math

import jax
import jax.numpy as jnp
from jax import lax
from jax.sharding import PartitionSpec as P

HD = 64


NEG = -1e30


def shards(
    video_query, video_kv, video_clip, audio_hidden, audio_qkv_weight, audio_clip, audio_out_weight
):
    audio_rows = audio_hidden.shape[0]
    width = video_query.shape[1]
    heads = width // HD
    local_rows = video_query.shape[0]
    block = math.gcd(local_rows, 512)
    blocks = local_rows // block
    quarters = lax.axis_size("seq") // 16
    position = lax.axis_index("seq")
    feature_group = position % 16
    quarter = position // 16
    local_weight = audio_qkv_weight[0]
    feature_count = local_weight.shape[0]
    columns = local_weight.shape[1]
    features = lax.dynamic_slice_in_dim(
        audio_hidden, feature_group * feature_count, feature_count, 1
    )
    rows = features
    partial_sum = jnp.dot(rows, local_weight, preferred_element_type=jnp.float32)
    padded = jnp.zeros((audio_rows, quarters * columns), jnp.float32)
    total = lax.psum(
        lax.dynamic_update_slice_in_dim(padded, partial_sum, quarter * columns, 1), "seq"
    )
    audio_qkv = total.astype(jnp.bfloat16)
    audio_qkv = audio_qkv.reshape(audio_rows, 3, heads, HD)
    audio_q = audio_qkv[:, 0]
    audio_k = audio_qkv[:, 1]
    audio_v = audio_qkv[:, 2]
    query_blocks = video_query.reshape(blocks, block, heads, HD)
    key_blocks = video_kv[0].reshape(blocks, block, heads, HD)
    value_blocks = video_kv[1].reshape(blocks, block, heads, HD)
    clip_blocks = video_clip.reshape(blocks, block)

    def video_block(inputs):
        query, clips = inputs
        same = (clips[:, None] == audio_clip[None, :])[None]
        scores = (
            jnp.einsum("bhd,khd->hbk", query, audio_k, preferred_element_type=jnp.float32) * 0.125
        )
        scores = jnp.where(same, scores, NEG)
        top = jnp.max(scores, axis=2, keepdims=True)
        expo = jnp.exp(scores - top)
        probs = (expo / jnp.sum(expo, axis=2, keepdims=True)).astype(jnp.bfloat16)
        result = jnp.einsum("hbk,khd->bhd", probs, audio_v, preferred_element_type=jnp.float32)
        return result.reshape(block, width).astype(jnp.bfloat16)

    video_attn = lax.map(video_block, (query_blocks, clip_blocks)).reshape(local_rows, width)

    def audio_block(state, inputs):
        top, total, numer = state
        key, value, clips = inputs
        same = (audio_clip[:, None] == clips[None, :])[:, None, :]
        scores = (
            jnp.einsum("ahd,bhd->ahb", audio_q, key, preferred_element_type=jnp.float32) * 0.125
        )
        scores = jnp.where(same, scores, NEG)
        new_top = jnp.maximum(top, jnp.max(scores, axis=2))
        weights = jnp.where(same, jnp.exp(scores - new_top[:, :, None]), jnp.float32(0.0))
        factor = jnp.exp(top - new_top)
        total = total * factor + jnp.sum(weights, axis=2)
        added = jnp.einsum(
            "ahb,bhd->ahd", weights.astype(jnp.bfloat16), value, preferred_element_type=jnp.float32
        )
        numer = numer.reshape(audio_rows, heads, HD) * factor[:, :, None] + added
        return ((new_top, total, numer.reshape(audio_rows, width)), None)

    start_state = (
        jnp.full((audio_rows, heads), NEG, jnp.float32),
        jnp.zeros((audio_rows, heads), jnp.float32),
        jnp.zeros((audio_rows, width), jnp.float32),
    )
    (top, total, numer), unused = lax.scan(
        audio_block, start_state, (key_blocks, value_blocks, clip_blocks)
    )
    global_top = lax.pmax(top, "seq")
    factor = jnp.exp(top - global_top)
    scaled = (numer.reshape(audio_rows, heads, HD) * factor[:, :, None]).reshape(audio_rows, width)
    numer_rows, total_rows = (
        lax.psum_scatter(scaled, "seq", scatter_dimension=0, tiled=True),
        lax.psum_scatter(total * factor, "seq", scatter_dimension=0, tiled=True),
    )
    share_rows = numer_rows.shape[0]
    finished = (numer_rows.reshape(share_rows, heads, HD) / total_rows[:, :, None]).reshape(
        share_rows, width
    )
    audio_attn = lax.all_gather(finished.astype(jnp.bfloat16), "seq", axis=0, tiled=True)
    rows = audio_attn
    audio_out = lax.psum_scatter(
        jnp.dot(rows, audio_out_weight, preferred_element_type=jnp.float32),
        "head",
        scatter_dimension=0,
        tiled=True,
    )
    return (video_attn, audio_out.astype(jnp.bfloat16))


def solution(mesh):
    return jax.shard_map(
        shards,
        mesh=mesh,
        in_specs=(
            P("seq", "head"),
            P(None, "seq", "head"),
            P("seq"),
            P(),
            P("seq", None, "head"),
            P(),
            P("head", "seq"),
        ),
        out_specs=(P("seq", "head"), P("head", "seq")),
        check_vma=False,
    )
```

profile of v0, /device:TPU:0, one launch (start us, length us, event | category | flops | bytes accessed | tf_op | source)
XLA Modules:
  0.0 714.0 jit_solution(9396893285349262931)
XLA Ops:
  7.3 3.4 broadcast_in_dim.64
  10.7 3.4 convolution_dynamic-update-slice_fusion
  14.1 122.9 %all-reduce.2 = bf16[256,6144]{1,0:T(8,128)(2,1)} all-reduce(f32[256,6144]{1,0:T(8,128)} %convolution_dynamic-update-slice_fusion), channel_id=1, replica_groups=mesh['seq'=32,'head'=1] {'seq'}, use_global_device_ids=true, to_apply=%region_0.1 | all-reduce | flops 1572864 | bytes 9437184 | tf_op jit(solution)/shard_map/psum | solution.py:36
  137.0 4.6 copy.26
  141.7 3.6 slice_bitcast_fusion
  145.3 12.0 %fusion.40 = (bf16[1,2048,2048]{2,1,0:T(8,128)(2,1)}, bf16[1,2048,2048]{2,1,0:T(8,128)(2,1)}) fusion(bf16[2,2048,2048]{2,1,0:T(8,128)(2,1)} %param.12), kind=kLoop, calls=%fused_computation.58 | loop fusion | bytes 33554432 | tf_op jit(solution)/shard_map/slice | solution.py:46
  157.2 24.4 %reshape.107 = bf16[4,512,32,64]{3,2,1,0:T(8,128)(2,1)} reshape(bf16[1,2048,2048]{2,1,0:T(8,128)(2,1)} %get-tuple-element.195) | data formatting | bytes 16777216 | tf_op jit(solution)/shard_map/reshape;squeeze | solution.py:45
  181.7 18.3 %copy.31 = bf16[4,512,32,64]{1,3,2,0:T(8,128)(2,1)} copy(bf16[4,512,32,64]{3,2,1,0:T(8,128)(2,1)} %reshape.107) | data formatting | bytes 16777216
  200.0 24.4 %reshape.108 = bf16[4,512,32,64]{3,2,1,0:T(8,128)(2,1)} reshape(bf16[1,2048,2048]{2,1,0:T(8,128)(2,1)} %get-tuple-element.194) | data formatting | bytes 16777216 | tf_op jit(solution)/shard_map/reshape;squeeze | solution.py:46
  224.5 18.3 %copy.32 = bf16[4,512,32,64]{1,3,2,0:T(8,128)(2,1)} copy(bf16[4,512,32,64]{3,2,1,0:T(8,128)(2,1)} %reshape.108) | data formatting | bytes 16777216
  244.3 115.9 %while.26 = (s32[]{:T(128)}, f32[256,32]{0,1:T(8,128)S(1)}, f32[256,32]{0,1:T(8,128)S(1)}, f32[256,2048]{0,1:T(8,128)}, s32[256]{0:T(256)S(1)}, /*index=5*/s32[4...) while((s32[]{:T(128)}, f32[256,32]{0,1:T(8,128)S(1)}, ...), condition=%wide.region_8.9_spmd.clone, body=%wide.region_5.8_spmd.clone.sunk | while | flops 1129488384 | bytes 127934616 | solution.py:87
  244.5 10.0 %fusion.67 = (f32[256,32]{0,1:T(8,128)S(1)}, f32[32,512,256]{2,1,0:T(8,128)}) fusion(pred[256,512]{0,1:T(8,128)(4,1)S(1)} %broadcast_compare_fusion.5, bf16[256,32,64]{0,2,1:T(8,128)(2,1)S(1)} %get-tuple-element.362, bf16[4,512,32,64]{1,3,2,0:T(8,128)(2,1)} %get-tuple-element.361, s32[]{:T(128)} %get-tuple-element.344), kind=kOutput, calls=%fused_computation.21.clone.1 | convolution fusion | flops 549445632 | bytes 20087296 | tf_op jit(solution)/shard_map/while/body/eval_jaxpr/ahd,bhd->ahb/dot_general | solution.py:69
  254.5 8.3 %fusion.68 = f32[256,32]{0,1:T(8,128)S(1)} fusion(f32[32,512,256]{2,1,0:T(8,128)} %get-tuple-element.306, f32[256,32]{0,1:T(8,128)S(1)} %select_maximum_fusion.2, pred[256,512]{0,1:T(8,128)(4,1)S(1)} %broadcast_compare_fusion.5), kind=kLoop, calls=%fused_computation.23.clone.1 | loop fusion | flops 20963328 | bytes 16973824 | tf_op jit(solution)/shard_map/while/body/eval_jaxpr/reduce_sum | solution.py:75
  265.2 8.1 %bitcast_add_fusion.2 = f32[256,32,64]{0,2,1:T(8,128)} fusion(f32[256,32,64]{0,2,1:T(8,128)} %bitcast.92, f32[32,512,256]{2,1,0:T(8,128)S(1)} %copy-done.2, f32[256,32]{0,1:T(8,128)S(1)} %select_maximum_fusion.2, pred[256,512]{0,1:T(8,128)(4,1)S(1)} %broadcast_compare_fusion.5, bf16[4,512,32,64]{1,3,2,0:T(8,128)(2,1)} %get-tuple-element.363, ...), kind=kOutput, calls=%fused_computation.26.clone.1 | convolution fusion | flops 558891008 | bytes 23265792 | tf_op jit(solution)/shard_map/while/body/eval_jaxpr/ahb,bhd->ahd/dot_general | solution.py:76
  273.4 10.0 %fusion.67 = (f32[256,32]{0,1:T(8,128)S(1)}, f32[32,512,256]{2,1,0:T(8,128)}) fusion(pred[256,512]{0,1:T(8,128)(4,1)S(1)} %broadcast_compare_fusion.5, bf16[256,32,64]{0,2,1:T(8,128)(2,1)S(1)} %get-tuple-element.362, bf16[4,512,32,64]{1,3,2,0:T(8,128)(2,1)} %get-tuple-element.361, s32[]{:T(128)} %get-tuple-element.344), kind=kOutput, calls=%fused_computation.21.clone.1 | convolution fusion | flops 549445632 | bytes 20087296 | tf_op jit(solution)/shard_map/while/body/eval_jaxpr/ahd,bhd->ahb/dot_general | solution.py:69
  283.5 8.3 %fusion.68 = f32[256,32]{0,1:T(8,128)S(1)} fusion(f32[32,512,256]{2,1,0:T(8,128)} %get-tuple-element.306, f32[256,32]{0,1:T(8,128)S(1)} %select_maximum_fusion.2, pred[256,512]{0,1:T(8,128)(4,1)S(1)} %broadcast_compare_fusion.5), kind=kLoop, calls=%fused_computation.23.clone.1 | loop fusion | flops 20963328 | bytes 16973824 | tf_op jit(solution)/shard_map/while/body/eval_jaxpr/reduce_sum | solution.py:75
  291.8 2.3 copy-done.2
  294.1 8.1 %bitcast_add_fusion.2 = f32[256,32,64]{0,2,1:T(8,128)} fusion(f32[256,32,64]{0,2,1:T(8,128)} %bitcast.92, f32[32,512,256]{2,1,0:T(8,128)S(1)} %copy-done.2, f32[256,32]{0,1:T(8,128)S(1)} %select_maximum_fusion.2, pred[256,512]{0,1:T(8,128)(4,1)S(1)} %broadcast_compare_fusion.5, bf16[4,512,32,64]{1,3,2,0:T(8,128)(2,1)} %get-tuple-element.363, ...), kind=kOutput, calls=%fused_computation.26.clone.1 | convolution fusion | flops 558891008 | bytes 23265792 | tf_op jit(solution)/shard_map/while/body/eval_jaxpr/ahb,bhd->ahd/dot_general | solution.py:76
  302.4 10.0 %fusion.67 = (f32[256,32]{0,1:T(8,128)S(1)}, f32[32,512,256]{2,1,0:T(8,128)}) fusion(pred[256,512]{0,1:T(8,128)(4,1)S(1)} %broadcast_compare_fusion.5, bf16[256,32,64]{0,2,1:T(8,128)(2,1)S(1)} %get-tuple-element.362, bf16[4,512,32,64]{1,3,2,0:T(8,128)(2,1)} %get-tuple-element.361, s32[]{:T(128)} %get-tuple-element.344), kind=kOutput, calls=%fused_computation.21.clone.1 | convolution fusion | flops 549445632 | bytes 20087296 | tf_op jit(solution)/shard_map/while/body/eval_jaxpr/ahd,bhd->ahb/dot_general | solution.py:69
  312.4 8.3 %fusion.68 = f32[256,32]{0,1:T(8,128)S(1)} fusion(f32[32,512,256]{2,1,0:T(8,128)} %get-tuple-element.306, f32[256,32]{0,1:T(8,128)S(1)} %select_maximum_fusion.2, pred[256,512]{0,1:T(8,128)(4,1)S(1)} %broadcast_compare_fusion.5), kind=kLoop, calls=%fused_computation.23.clone.1 | loop fusion | flops 20963328 | bytes 16973824 | tf_op jit(solution)/shard_map/while/body/eval_jaxpr/reduce_sum | solution.py:75
  320.8 2.3 copy-done.2
  323.1 8.1 %bitcast_add_fusion.2 = f32[256,32,64]{0,2,1:T(8,128)} fusion(f32[256,32,64]{0,2,1:T(8,128)} %bitcast.92, f32[32,512,256]{2,1,0:T(8,128)S(1)} %copy-done.2, f32[256,32]{0,1:T(8,128)S(1)} %select_maximum_fusion.2, pred[256,512]{0,1:T(8,128)(4,1)S(1)} %broadcast_compare_fusion.5, bf16[4,512,32,64]{1,3,2,0:T(8,128)(2,1)} %get-tuple-element.363, ...), kind=kOutput, calls=%fused_computation.26.clone.1 | convolution fusion | flops 558891008 | bytes 23265792 | tf_op jit(solution)/shard_map/while/body/eval_jaxpr/ahb,bhd->ahd/dot_general | solution.py:76
  331.4 10.0 %fusion.67 = (f32[256,32]{0,1:T(8,128)S(1)}, f32[32,512,256]{2,1,0:T(8,128)}) fusion(pred[256,512]{0,1:T(8,128)(4,1)S(1)} %broadcast_compare_fusion.5, bf16[256,32,64]{0,2,1:T(8,128)(2,1)S(1)} %get-tuple-element.362, bf16[4,512,32,64]{1,3,2,0:T(8,128)(2,1)} %get-tuple-element.361, s32[]{:T(128)} %get-tuple-element.344), kind=kOutput, calls=%fused_computation.21.clone.1 | convolution fusion | flops 549445632 | bytes 20087296 | tf_op jit(solution)/shard_map/while/body/eval_jaxpr/ahd,bhd->ahb/dot_general | solution.py:69
  341.4 8.3 %fusion.68 = f32[256,32]{0,1:T(8,128)S(1)} fusion(f32[32,512,256]{2,1,0:T(8,128)} %get-tuple-element.306, f32[256,32]{0,1:T(8,128)S(1)} %select_maximum_fusion.2, pred[256,512]{0,1:T(8,128)(4,1)S(1)} %broadcast_compare_fusion.5), kind=kLoop, calls=%fused_computation.23.clone.1 | loop fusion | flops 20963328 | bytes 16973824 | tf_op jit(solution)/shard_map/while/body/eval_jaxpr/reduce_sum | solution.py:75
  352.1 8.1 %bitcast_add_fusion.2 = f32[256,32,64]{0,2,1:T(8,128)} fusion(f32[256,32,64]{0,2,1:T(8,128)} %bitcast.92, f32[32,512,256]{2,1,0:T(8,128)S(1)} %copy-done.2, f32[256,32]{0,1:T(8,128)S(1)} %select_maximum_fusion.2, pred[256,512]{0,1:T(8,128)(4,1)S(1)} %broadcast_compare_fusion.5, bf16[4,512,32,64]{1,3,2,0:T(8,128)(2,1)} %get-tuple-element.363, ...), kind=kOutput, calls=%fused_computation.26.clone.1 | convolution fusion | flops 558891008 | bytes 23265792 | tf_op jit(solution)/shard_map/while/body/eval_jaxpr/ahb,bhd->ahd/dot_general | solution.py:76
  360.2 37.4 %pmax.7 = f32[256,32]{0,1:T(8,128)S(1)} all-reduce(f32[256,32]{0,1:T(8,128)S(1)} %get-tuple-element.90), channel_id=1, replica_groups=mesh['seq'=32,'head'=1] {'seq'}, use_global_device_ids=true, to_apply=%region_9.10 | all-reduce | flops 8192 | bytes 65536 | tf_op jit(solution)/shard_map/pmax | solution.py:90
  401.3 24.5 %reshape.106 = bf16[4,512,32,64]{3,2,1,0:T(8,128)(2,1)} reshape(bf16[2048,2048]{1,0:T(8,128)(2,1)} %param.11) | data formatting | bytes 16777216 | tf_op jit(solution)/shard_map/reshape | solution.py:44
  425.8 18.4 %copy.27 = bf16[4,512,32,64]{1,3,2,0:T(8,128)(2,1)} copy(bf16[4,512,32,64]{3,2,1,0:T(8,128)(2,1)} %reshape.106) | data formatting | bytes 16777216 | tf_op jit(solution)/shard_map/while | solution.py:62
  444.2 41.4 %all-reduce = f32[256,32]{0,1:T(8,128)S(1)} all-reduce(f32[256,32]{0,1:T(8,128)S(1)} %get-tuple-element.188), channel_id=3, replica_groups=mesh['seq'=32,'head'=1] {'seq'}, use_global_device_ids=true, to_apply=%region_11.12.clone | all-reduce | flops 8192 | bytes 65536
  485.7 54.0 %reduce-scatter.5.cloned.1.call-done = f32[8,2048]{1,0:T(8,128)} async-done(((f32[256,2048]{1,0:T(8,128)}), f32[8,2048]{1,0:T(8,128)}) %reduce-scatter.5.cloned.1.call-update) | async-done | bytes 65552
  541.8 162.9 %while.25 = (s32[]{:T(128)}, bf16[4,512,2048]{2,1,0:T(8,128)(2,1)}, s32[4,512]{1,0:T(4,128)S(1)}, s32[256]{0:T(256)S(1)}, bf16[4,512,32,64]{1,3,2,0:T(8,128)(2,1...) while((s32[]{:T(128)}, bf16[4,512,2048]{2,1,0:T(8,128)(2,1)}, ...), condition=%wide.region_4.5_spmd, body=%wide.region_1.4_spmd.sunk | while | flops 1108476160 | bytes 86384760 | solution.py:62
  541.9 9.7 %fusion.61 = f32[32,512,256]{1,2,0:T(8,128)} fusion(bf16[256,32,64]{0,2,1:T(8,128)(2,1)S(1)} %get-tuple-element.330, bf16[4,512,32,64]{1,3,2,0:T(8,128)(2,1)} %get-tuple-element.329, s32[]{:T(128)} %get-tuple-element.317), kind=kOutput, calls=%fused_computation.9.clone.1 | convolution fusion | flops 536870912 | bytes 19923456 | tf_op jit(solution)/shard_map/while/body/eval_jaxpr/bhd,khd->hbk/dot_general | solution.py:53
  551.7 17.7 %fusion.62 = (f32[32,512]{1,0:T(8,128)S(1)}, f32[32,512,256]{1,2,0:T(8,128)}) fusion(f32[32,512,256]{1,2,0:T(8,128)} %fusion.61, pred[512,256]{0,1:T(8,128)(4,1)S(1)} %broadcast_compare_fusion.4), kind=kOutput, calls=%fused_computation.57.clone.1 | output fusion | flops 25166080 | bytes 33751040 | tf_op jit(solution)/shard_map/while/body/eval_jaxpr/sub | solution.py:57
  569.5 8.8 %fusion.63 = bf16[32,512,64]{1,2,0:T(8,128)(2,1)} fusion(bf16[256,32,64]{0,2,1:T(8,128)(2,1)S(1)} %copy-done.4, f32[32,512,256]{1,2,0:T(8,128)} %get-tuple-element.294, f32[32,512]{1,0:T(8,128)S(1)} %get-tuple-element.295), kind=kOutput, calls=%fused_computation.12.clone.1 | convolution fusion | flops 546308096 | bytes 19988480 | tf_op jit(solution)/shard_map/while/body/eval_jaxpr/hbk,khd->bhd/dot_general | solution.py:59
  578.3 2.9 copy.49
  582.7 9.7 %fusion.61 = f32[32,512,256]{1,2,0:T(8,128)} fusion(bf16[256,32,64]{0,2,1:T(8,128)(2,1)S(1)} %get-tuple-element.330, bf16[4,512,32,64]{1,3,2,0:T(8,128)(2,1)} %get-tuple-element.329, s32[]{:T(128)} %get-tuple-element.317), kind=kOutput, calls=%fused_computation.9.clone.1 | convolution fusion | flops 536870912 | bytes 19923456 | tf_op jit(solution)/shard_map/while/body/eval_jaxpr/bhd,khd->hbk/dot_general | solution.py:53
  592.5 17.7 %fusion.62 = (f32[32,512]{1,0:T(8,128)S(1)}, f32[32,512,256]{1,2,0:T(8,128)}) fusion(f32[32,512,256]{1,2,0:T(8,128)} %fusion.61, pred[512,256]{0,1:T(8,128)(4,1)S(1)} %broadcast_compare_fusion.4), kind=kOutput, calls=%fused_computation.57.clone.1 | output fusion | flops 25166080 | bytes 33751040 | tf_op jit(solution)/shard_map/while/body/eval_jaxpr/sub | solution.py:57
  610.2 8.8 %fusion.63 = bf16[32,512,64]{1,2,0:T(8,128)(2,1)} fusion(bf16[256,32,64]{0,2,1:T(8,128)(2,1)S(1)} %copy-done.4, f32[32,512,256]{1,2,0:T(8,128)} %get-tuple-element.294, f32[32,512]{1,0:T(8,128)S(1)} %get-tuple-element.295), kind=kOutput, calls=%fused_computation.12.clone.1 | convolution fusion | flops 546308096 | bytes 19988480 | tf_op jit(solution)/shard_map/while/body/eval_jaxpr/hbk,khd->bhd/dot_general | solution.py:59
  619.0 2.9 copy.49
  623.4 9.7 %fusion.61 = f32[32,512,256]{1,2,0:T(8,128)} fusion(bf16[256,32,64]{0,2,1:T(8,128)(2,1)S(1)} %get-tuple-element.330, bf16[4,512,32,64]{1,3,2,0:T(8,128)(2,1)} %get-tuple-element.329, s32[]{:T(128)} %get-tuple-element.317), kind=kOutput, calls=%fused_computation.9.clone.1 | convolution fusion | flops 536870912 | bytes 19923456 | tf_op jit(solution)/shard_map/while/body/eval_jaxpr/bhd,khd->hbk/dot_general | solution.py:53
  633.2 17.7 %fusion.62 = (f32[32,512]{1,0:T(8,128)S(1)}, f32[32,512,256]{1,2,0:T(8,128)}) fusion(f32[32,512,256]{1,2,0:T(8,128)} %fusion.61, pred[512,256]{0,1:T(8,128)(4,1)S(1)} %broadcast_compare_fusion.4), kind=kOutput, calls=%fused_computation.57.clone.1 | output fusion | flops 25166080 | bytes 33751040 | tf_op jit(solution)/shard_map/while/body/eval_jaxpr/sub | solution.py:57
  650.9 8.8 %fusion.63 = bf16[32,512,64]{1,2,0:T(8,128)(2,1)} fusion(bf16[256,32,64]{0,2,1:T(8,128)(2,1)S(1)} %copy-done.4, f32[32,512,256]{1,2,0:T(8,128)} %get-tuple-element.294, f32[32,512]{1,0:T(8,128)S(1)} %get-tuple-element.295), kind=kOutput, calls=%fused_computation.12.clone.1 | convolution fusion | flops 546308096 | bytes 19988480 | tf_op jit(solution)/shard_map/while/body/eval_jaxpr/hbk,khd->bhd/dot_general | solution.py:59
  659.7 2.9 copy.49
  664.1 9.7 %fusion.61 = f32[32,512,256]{1,2,0:T(8,128)} fusion(bf16[256,32,64]{0,2,1:T(8,128)(2,1)S(1)} %get-tuple-element.330, bf16[4,512,32,64]{1,3,2,0:T(8,128)(2,1)} %get-tuple-element.329, s32[]{:T(128)} %get-tuple-element.317), kind=kOutput, calls=%fused_computation.9.clone.1 | convolution fusion | flops 536870912 | bytes 19923456 | tf_op jit(solution)/shard_map/while/body/eval_jaxpr/bhd,khd->hbk/dot_general | solution.py:53
  673.9 17.7 %fusion.62 = (f32[32,512]{1,0:T(8,128)S(1)}, f32[32,512,256]{1,2,0:T(8,128)}) fusion(f32[32,512,256]{1,2,0:T(8,128)} %fusion.61, pred[512,256]{0,1:T(8,128)(4,1)S(1)} %broadcast_compare_fusion.4), kind=kOutput, calls=%fused_computation.57.clone.1 | output fusion | flops 25166080 | bytes 33751040 | tf_op jit(solution)/shard_map/while/body/eval_jaxpr/sub | solution.py:57
  691.6 8.8 %fusion.63 = bf16[32,512,64]{1,2,0:T(8,128)(2,1)} fusion(bf16[256,32,64]{0,2,1:T(8,128)(2,1)S(1)} %copy-done.4, f32[32,512,256]{1,2,0:T(8,128)} %get-tuple-element.294, f32[32,512]{1,0:T(8,128)S(1)} %get-tuple-element.295), kind=kOutput, calls=%fused_computation.12.clone.1 | convolution fusion | flops 546308096 | bytes 19988480 | tf_op jit(solution)/shard_map/while/body/eval_jaxpr/hbk,khd->bhd/dot_general | solution.py:59
  700.4 2.9 copy.49
  704.8 2.4 convolution_convert_fusion
  (75 shorter events, 19.2 us)
Async XLA Ops:
  7.2 3.6 copy-start
  7.2 532.5 %reduce-scatter.5.cloned.1.call-start = ((), (), s32[]{:S(2)}) async-start(), calls=%async_computation.2 | async-start | bytes 2162688
  224.5 18.3 %copy-start.7 = (s32[2048]{0:T(1024)S(1)}, s32[2048]{0:T(1024)}, u32[]{:S(2)}) copy-start(s32[2048]{0:T(1024)} %param.13) | copy-start | bytes 24580
  224.5 19.9 %copy-start.6 = (s32[256]{0:T(256)S(1)}, s32[256]{0:T(256)}, u32[]{:S(2)}) copy-start(s32[256]{0:T(256)} %param.16) | copy-start | bytes 3076
  254.5 10.7 %copy-start.2 = (f32[32,512,256]{2,1,0:T(8,128)S(1)}, f32[32,512,256]{2,1,0:T(8,128)}, u32[]{:S(2)}) copy-start(f32[32,512,256]{2,1,0:T(8,128)} %get-tuple-element.306) | copy-start | bytes 50331652 | tf_op jit(solution)/shard_map/while
  283.5 10.7 %copy-start.2 = (f32[32,512,256]{2,1,0:T(8,128)S(1)}, f32[32,512,256]{2,1,0:T(8,128)}, u32[]{:S(2)}) copy-start(f32[32,512,256]{2,1,0:T(8,128)} %get-tuple-element.306) | copy-start | bytes 50331652 | tf_op jit(solution)/shard_map/while
  312.4 10.7 %copy-start.2 = (f32[32,512,256]{2,1,0:T(8,128)S(1)}, f32[32,512,256]{2,1,0:T(8,128)}, u32[]{:S(2)}) copy-start(f32[32,512,256]{2,1,0:T(8,128)} %get-tuple-element.306) | copy-start | bytes 50331652 | tf_op jit(solution)/shard_map/while
  341.4 10.7 %copy-start.2 = (f32[32,512,256]{2,1,0:T(8,128)S(1)}, f32[32,512,256]{2,1,0:T(8,128)}, u32[]{:S(2)}) copy-start(f32[32,512,256]{2,1,0:T(8,128)} %get-tuple-element.306) | copy-start | bytes 50331652 | tf_op jit(solution)/shard_map/while
  401.3 303.5 %all-gather.2.cloned.1.call-start = ((), (), s32[]{:S(2)}) async-start(), calls=%async_computation.1 | async-start | bytes 1081344 | tf_op jit(solution)/shard_map/all_gather | solution.py:101
  425.8 116.0 %copy-start.3 = (bf16[256,32,64]{0,2,1:T(8,128)(2,1)S(1)}, bf16[256,32,64]{0,2,1:T(8,128)(2,1)}, u32[]{:S(2)}) copy-start(bf16[256,32,64]{0,2,1:T(8,128)(2,1)} %get-tuple-element.314) | copy-start | bytes 3145732
  541.8 163.0 %copy-start.5 = (bf16[2048,64]{0,1:T(8,128)(2,1)S(1)}, bf16[2048,64]{0,1:T(8,128)(2,1)}, u32[]{:S(2)}) copy-start(bf16[2048,64]{0,1:T(8,128)(2,1)} %param.17) | copy-start | bytes 786436
  551.7 17.7 %copy-start.4 = (bf16[256,32,64]{0,2,1:T(8,128)(2,1)S(1)}, bf16[256,32,64]{0,2,1:T(8,128)(2,1)}, u32[]{:S(2)}) copy-start(bf16[256,32,64]{0,2,1:T(8,128)(2,1)} %get-tuple-element.331) | copy-start | bytes 3145732 | tf_op jit(solution)/shard_map/while
  592.5 17.7 %copy-start.4 = (bf16[256,32,64]{0,2,1:T(8,128)(2,1)S(1)}, bf16[256,32,64]{0,2,1:T(8,128)(2,1)}, u32[]{:S(2)}) copy-start(bf16[256,32,64]{0,2,1:T(8,128)(2,1)} %get-tuple-element.331) | copy-start | bytes 3145732 | tf_op jit(solution)/shard_map/while
  633.2 17.7 %copy-start.4 = (bf16[256,32,64]{0,2,1:T(8,128)(2,1)S(1)}, bf16[256,32,64]{0,2,1:T(8,128)(2,1)}, u32[]{:S(2)}) copy-start(bf16[256,32,64]{0,2,1:T(8,128)(2,1)} %get-tuple-element.331) | copy-start | bytes 3145732 | tf_op jit(solution)/shard_map/while
  673.9 17.7 %copy-start.4 = (bf16[256,32,64]{0,2,1:T(8,128)(2,1)S(1)}, bf16[256,32,64]{0,2,1:T(8,128)(2,1)}, u32[]{:S(2)}) copy-start(bf16[256,32,64]{0,2,1:T(8,128)(2,1)} %get-tuple-element.331) | copy-start | bytes 3145732 | tf_op jit(solution)/shard_map/while
  704.8 2.4 copy-start.1
Sparse Core Ops, SparseCore 0:
  401.4 138.2 reduce-scatter.4
  543.2 49.4 all-gather.1
where the time goes:
time: 718 us; the launch traced here: 714 us
  blocking collectives  202 us (28%)
  local copies, waits for them, and re-layouts  184 us (26%)
  matrix products  152 us (21%)
  other arithmetic  107 us (15%)
  waiting for transfers between devices  54.1 us (8%)
  between operations  14.2 us (2%)
    psum x1, blocking collectives, shards(): lax.psum(lax.dynamic_update_slice_in_dim(padded, partial_sum, quarter * c...  123 us
    sub x4, other arithmetic, video_block(): expo = jnp.exp(scores - top)  70.8 us
    unnamed x3, waiting for transfers between devices  54.1 us
    unnamed x1, blocking collectives  41.4 us
    dot_general x4, matrix products, audio_block(): jnp.einsum('ahd,bhd->ahb', audio_q, key, preferred_element_type=jnp.float32)  40 us
    unnamed x17, local copies, waits for them, and re-layouts  39.8 us
    dot_general x4, matrix products, video_block(): jnp.einsum('bhd,khd->hbk', query, audio_k, preferred_element_type=jnp.flo...  38.8 us
    pmax x1, blocking collectives, shards(): global_top = lax.pmax(top, 'seq')  37.4 us
  transfers between devices with their start and end apart: 2, of which 1 were waited for; matrix products, arithmetic and copies ran while one was open for 29% of the time, Pallas kernels for 0%

commit v1 on v0

v1 whole, which is shorter than its diff:
```python
import functools

import jax
import jax.numpy as jnp
from jax import lax
from jax.experimental import pallas as pl
from jax.experimental.pallas import tpu as pltpu
from jax.sharding import PartitionSpec as P

HD = 64
PAIR = 2 * HD
GROUP = 16
NEG = -1e30
NT = (((1,), (1,)), ((), ()))
SMEM = pl.BlockSpec(memory_space=pltpu.SMEM)


def pick_kernel(where_ref, weight_ref, out_ref):
    members, _, features = out_ref.shape
    quarter = where_ref[0]
    wide = weight_ref.shape[1] // PAIR * 2 // 3
    wide_start = quarter * (wide // 2)
    keys_start = (1 - quarter) * wide
    for member in range(members):
        lanes = pl.ds(pl.multiple_of((wide_start + member) * PAIR, PAIR), PAIR)
        out_ref[member, :PAIR, :] = weight_ref[:, lanes].T
    for two in range(members // 2):
        lanes = pl.ds(pl.multiple_of((keys_start + two) * PAIR, PAIR), PAIR)
        keys = weight_ref[:, lanes].T
        out_ref[2 * two, PAIR:, :] = keys[:HD]
        out_ref[2 * two + 1, PAIR:, :] = keys[HD:]


def project_kernel(weight_ref, hidden_ref, out_ref):
    members, _, features = weight_ref.shape
    total = None
    for member in range(members):
        part = lax.dot_general(
            weight_ref[member],
            hidden_ref[:, member * features : (member + 1) * features],
            NT,
            preferred_element_type=jnp.float32,
        )
        total = part if total is None else total + part
    out_ref[...] = total.astype(out_ref.dtype)


def fill_bias(bias_ref, audio_clip_ref, video_clip_ref):
    bias_ref[...] = jnp.where(
        audio_clip_ref[...] == video_clip_ref[...], jnp.float32(0.0), jnp.float32(NEG)
    )


def audio_kernel(
    table_ref, video_clip_ref, audio_clip_ref, qkv_ref, key_ref, value_ref,
    send_ref, keep_ref, bias_ref, values_ref, *, pairs
):
    step = pl.program_id(0)
    half = send_ref.shape[0]
    width = pairs * PAIR

    @pl.when(step == 0)
    def _():
        fill_bias(bias_ref, audio_clip_ref, video_clip_ref)
        values_ref[:, PAIR:] = jnp.ones((values_ref.shape[0], PAIR), values_ref.dtype)
        send_ref[:, width:] = jnp.zeros((half, PAIR), jnp.float32)
        keep_ref[:, width:] = jnp.zeros((half, PAIR), jnp.float32)

    values_ref[:, :PAIR] = value_ref[0]
    first = pl.multiple_of(table_ref[step], HD)
    query = qkv_ref[pl.ds(first, PAIR), :] * jnp.bfloat16(0.125)
    row = lax.broadcasted_iota(jnp.int32, query.shape, 0)
    lane = lax.broadcasted_iota(jnp.int32, (2 * half, PAIR), 1)
    outs, stats = [], None
    for h in range(2):
        own = (row >= HD) if h else (row < HD)
        query_h = jnp.where(own, query, jnp.zeros_like(query)).T
        scores = lax.dot_general(query_h, key_ref[0], NT, preferred_element_type=jnp.float32)
        scores = scores + bias_ref[...]
        top = jnp.max(scores, axis=1, keepdims=True)
        weights = jnp.exp(scores - top).astype(jnp.bfloat16)
        out = jnp.dot(weights, values_ref[...], preferred_element_type=jnp.float32)
        outs.append(out[:, :PAIR])
        head = 2 * step + h
        mine = jnp.where(lane == head, top, jnp.where(lane == head + HD, out[:, PAIR:], 0.0))
        stats = mine if stats is None else stats + mine
    numer = jnp.where(lane < HD, outs[0], outs[1])
    lanes = pl.ds(pl.multiple_of(step * PAIR, PAIR), PAIR)
    upper = table_ref[4 * pairs] == 1
    keep_ref[:, lanes] = jnp.where(upper, numer[half:], numer[:half])
    send_ref[:, lanes] = jnp.where(upper, numer[:half], numer[half:])
    keep_ref[:, width:] += jnp.where(upper, stats[half:], stats[:half])
    send_ref[:, width:] += jnp.where(upper, stats[:half], stats[half:])


def audio_partials(table, video_clip, audio_clip, qkv, video_kv):
    rows = qkv.shape[1]
    _, length, width = video_kv.shape
    pairs = width // PAIR
    half = jax.ShapeDtypeStruct((rows // 2, width + PAIR), jnp.float32)
    half_spec = pl.BlockSpec((rows // 2, width + PAIR), lambda p, t: (0, 0))
    return pl.pallas_call(
        functools.partial(audio_kernel, pairs=pairs),
        grid_spec=pltpu.PrefetchScalarGridSpec(
            num_scalar_prefetch=1,
            grid=(pairs,),
            in_specs=[
                pl.BlockSpec((1, length), lambda p, t: (0, 0)),
                pl.BlockSpec((rows, 1), lambda p, t: (0, 0)),
                pl.BlockSpec(qkv.shape, lambda p, t: (0, 0)),
                pl.BlockSpec((1, length, PAIR), lambda p, t: (0, 0, p)),
                pl.BlockSpec((1, length, PAIR), lambda p, t: (1, 0, p)),
            ],
            out_specs=[half_spec, half_spec],
            scratch_shapes=[
                pltpu.VMEM((rows, length), jnp.float32),
                pltpu.VMEM((length, 2 * PAIR), jnp.bfloat16),
            ],
        ),
        out_shape=[half, half],
        name="audio_partials",
    )(table, video_clip, audio_clip, qkv, video_kv, video_kv)


def video_kernel(
    table_ref, video_clip_ref, audio_clip_ref, qkv_ref, query_ref, out_ref, bias_ref,
    *, pairs, block
):
    step = pl.program_id(0)
    rows = qkv_ref.shape[1]

    @pl.when(step == 0)
    def _():
        fill_bias(bias_ref, audio_clip_ref, video_clip_ref)

    value_start = pl.multiple_of(table_ref[3 * pairs + step], HD)
    blank = jnp.zeros((HD, rows), jnp.bfloat16)
    ones = jnp.ones((16, rows), jnp.bfloat16)
    keys, values = [], []
    for h in range(2):
        key_start = pl.multiple_of(table_ref[pairs + 2 * step + h], HD)
        key = qkv_ref[pl.ds(key_start, HD), :] * jnp.bfloat16(0.125)
        keys.append(jnp.concatenate([blank, key] if h else [key, blank], axis=0).T)
        value = qkv_ref[pl.ds(value_start + h * HD, HD), :]
        values.append(jnp.concatenate([value, ones], axis=0))
    for start in range(0, query_ref.shape[0], block):
        columns = slice(start, start + block)
        outs = []
        for h in range(2):
            scores = lax.dot_general(
                keys[h], query_ref[columns, :], NT, preferred_element_type=jnp.float32
            )
            scores = scores + bias_ref[:, columns]
            top = jnp.max(scores, axis=0, keepdims=True)
            weights = jnp.exp(scores - top).astype(jnp.bfloat16)
            out = jnp.dot(values[h], weights, preferred_element_type=jnp.float32)
            outs.append(out[:HD] * (1.0 / out[HD : HD + 1]))
        out_ref[columns, :] = jnp.concatenate(outs, axis=0).T.astype(out_ref.dtype)


def video_attend(table, video_clip, audio_clip, qkv, video_query, block=512):
    rows = qkv.shape[1]
    length, width = video_query.shape
    pairs = width // PAIR
    return pl.pallas_call(
        functools.partial(video_kernel, pairs=pairs, block=block),
        grid_spec=pltpu.PrefetchScalarGridSpec(
            num_scalar_prefetch=1,
            grid=(pairs,),
            in_specs=[
                pl.BlockSpec((1, length), lambda p, t: (0, 0)),
                pl.BlockSpec((rows, 1), lambda p, t: (0, 0)),
                pl.BlockSpec(qkv.shape, lambda p, t: (0, 0)),
                pl.BlockSpec((length, PAIR), lambda p, t: (0, p)),
            ],
            out_specs=pl.BlockSpec((length, PAIR), lambda p, t: (0, p)),
            scratch_shapes=[pltpu.VMEM((rows, length), jnp.float32)],
        ),
        out_shape=jax.ShapeDtypeStruct((length, width), jnp.bfloat16),
        name="video_attend",
    )(table, video_clip, audio_clip, qkv, video_query)


def merged(keep_ref, other_ref, rows, width):
    mine, theirs = keep_ref[rows, width:], other_ref[rows, width:]
    top = jnp.maximum(mine, theirs)
    mine_by, theirs_by = jnp.exp(mine - top), jnp.exp(theirs - top)
    total = mine * pltpu.roll(mine_by, HD, 1) + theirs * pltpu.roll(theirs_by, HD, 1)
    lane = lax.broadcasted_iota(jnp.int32, top.shape, 1)
    stats = jnp.where(lane < HD, top, total)

    def numerator(pair):
        lanes = slice(pair * PAIR, (pair + 1) * PAIR)

        def spread(by):
            two = slice(2 * pair, 2 * pair + 1), slice(2 * pair + 1, 2 * pair + 2)
            return jnp.where(lane < HD, by[:, two[0]], by[:, two[1]])

        return keep_ref[rows, lanes] * spread(mine_by) + other_ref[rows, lanes] * spread(theirs_by)

    return numerator, stats


def merge_kernel(bit_ref, keep_ref, other_ref, send_ref, next_ref):
    half, width = send_ref.shape[0], send_ref.shape[1] - PAIR
    bit = bit_ref[0]
    for out_ref, part in ((send_ref, 1 - bit), (next_ref, bit)):
        rows = pl.ds(pl.multiple_of(part * half, half), half)
        numerator, stats = merged(keep_ref, other_ref, rows, width)
        for pair in range(width // PAIR):
            out_ref[:, pair * PAIR : (pair + 1) * PAIR] = numerator(pair)
        out_ref[:, width:] = stats


def finish_kernel(keep_ref, other_ref, out_ref):
    width = out_ref.shape[1]
    numerator, stats = merged(keep_ref, other_ref, slice(None), width)
    lane = lax.broadcasted_iota(jnp.int32, stats.shape, 1)
    for pair in range(width // PAIR):
        first = HD + 2 * pair
        total = jnp.where(lane < HD, stats[:, first : first + 1], stats[:, first + 1 : first + 2])
        out_ref[:, pair * PAIR : (pair + 1) * PAIR] = (numerator(pair) / total).astype(out_ref.dtype)


def mirrored(index, size):
    result = 0 * index
    for bit in range(size.bit_length() - 1):
        result = 2 * result + index // (1 << bit) % 2
    return result


def out_kernel(position_ref, attn_ref, weight_ref, out_ref, rows_ref, *, size):
    share = attn_ref.shape[0] // size
    position = position_ref[0]
    result = jnp.dot(attn_ref[...], weight_ref[...], preferred_element_type=jnp.float32)
    for block in range(size):
        start, bit, length = 0, 1, attn_ref.shape[0]
        device = position ^ mirrored(block, size)
        while bit < size:
            length //= 2
            start = start + (device // bit % 2) * length
            bit *= 2
        rows_ref[pl.ds(pl.multiple_of(start, share), share), :] = result[
            block * share : (block + 1) * share
        ]
    out_ref[...] = rows_ref[...].astype(out_ref.dtype)


def swap(array, bit, size):
    return lax.ppermute(array, "seq", [(i, i ^ bit) for i in range(size)])


def gathered(array, size):
    bits = [1 << k for k in range(size.bit_length() - 1)]
    ordered = array
    for bit in reversed(bits):
        ordered = jnp.concatenate([ordered[None], swap(ordered, bit, size)[None]], axis=0)
    ordered = ordered.reshape((2,) * len(bits) + array.shape)
    return ordered.reshape((size * array.shape[0],) + array.shape[1:])


def projected_parts(position, audio_hidden, weight, size):
    features, columns = weight.shape
    rows = audio_hidden.shape[0]
    share = columns // GROUP
    picked = pl.pallas_call(
        pick_kernel,
        in_specs=[SMEM, pl.BlockSpec(memory_space=pltpu.VMEM)],
        out_shape=jax.ShapeDtypeStruct((GROUP, share, features), weight.dtype),
        name="pick",
    )((position // GROUP)[None], weight)
    groups = [list(range(s, s + GROUP)) for s in range(0, size, GROUP)]
    own = lax.all_to_all(picked, "seq", 0, 0, axis_index_groups=groups)
    part = pl.pallas_call(
        project_kernel,
        out_shape=jax.ShapeDtypeStruct((share, rows), jnp.bfloat16),
        name="project",
    )(own, audio_hidden)
    qkv = gathered(part, size)
    blocks = mirrored(position ^ jnp.arange(size), size) * share
    return qkv, jnp.concatenate([blocks[:GROUP], blocks + PAIR, blocks[GROUP:]])


def projected_whole(position, audio_hidden, weight, size):
    features, columns = weight.shape
    rows = audio_hidden.shape[0]
    quarters = size // GROUP
    mine = lax.dynamic_slice_in_dim(audio_hidden, position % GROUP * features, features, 1)
    part = jnp.dot(mine, weight, preferred_element_type=jnp.float32)
    padded = jnp.zeros((rows, quarters * columns), jnp.float32)
    placed = lax.dynamic_update_slice_in_dim(padded, part, position // GROUP * columns, 1)
    qkv = lax.psum(placed, "seq").astype(jnp.bfloat16).T
    width = quarters * columns // 3
    queries = jnp.arange(0, width, PAIR)
    keys = jnp.arange(width, 2 * width, HD)
    return qkv, jnp.concatenate([queries, keys, 2 * width + queries])


def finished_rows(position, send, keep, size):
    bit = 1
    while bit < size:
        other = swap(send, bit, size)
        bit *= 2
        shape = (keep.shape[0] // 2, keep.shape[1])
        if bit < size:
            send, keep = pl.pallas_call(
                merge_kernel,
                in_specs=[SMEM] + [pl.BlockSpec(memory_space=pltpu.VMEM)] * 2,
                out_shape=[jax.ShapeDtypeStruct(shape, jnp.float32)] * 2,
                name="merge",
            )((position // bit % 2)[None], keep, other)
    return pl.pallas_call(
        finish_kernel,
        out_shape=jax.ShapeDtypeStruct((keep.shape[0], keep.shape[1] - PAIR), jnp.bfloat16),
        name="finish",
    )(keep, other)


def whole_rows(position, send, keep, size):
    first = position % 2 == 0
    both = jnp.where(
        first, jnp.concatenate([keep, send], axis=0), jnp.concatenate([send, keep], axis=0)
    )
    width = both.shape[1] - PAIR
    heads = width // HD
    numer = both[:, :width].reshape(-1, heads, HD)
    top, total = both[:, width : width + heads], both[:, width + HD : width + HD + heads]
    factor = jnp.exp(top - lax.pmax(top, "seq"))
    numer = lax.psum_scatter(
        (numer * factor[:, :, None]).reshape(-1, width), "seq", scatter_dimension=0, tiled=True
    )
    total = lax.psum_scatter(total * factor, "seq", scatter_dimension=0, tiled=True)
    done = (numer.reshape(-1, heads, HD) / total[:, :, None]).reshape(-1, width)
    return lax.all_gather(done.astype(jnp.bfloat16), "seq", axis=0, tiled=True)


def shards(
    video_query, video_kv, video_clip, audio_hidden, audio_qkv_weight, audio_clip, audio_out_weight
):
    size = lax.axis_size("seq")
    position = lax.axis_index("seq")
    rows = audio_hidden.shape[0]
    width = video_query.shape[1]
    pairs = width // PAIR
    halves = size == 2 * GROUP and pairs == GROUP
    project = projected_parts if halves else projected_whole
    qkv, starts = project(position, audio_hidden, audio_qkv_weight[0], size)
    table = jnp.concatenate([starts, (position % 2)[None]]).astype(jnp.int32)
    clips = video_clip[None], audio_clip[:, None]
    send, keep = audio_partials(table, *clips, qkv, video_kv)
    video_attn = video_attend(table, *clips, qkv, video_query)
    if rows % (8 * size) == 0 and lax.axis_size("head") == 1:
        attn = gathered(finished_rows(position, send, keep, size), size)
        audio_out = pl.pallas_call(
            functools.partial(out_kernel, size=size),
            in_specs=[SMEM] + [pl.BlockSpec(memory_space=pltpu.VMEM)] * 2,
            out_shape=jax.ShapeDtypeStruct((rows, audio_out_weight.shape[1]), jnp.bfloat16),
            scratch_shapes=[pltpu.VMEM((rows, audio_out_weight.shape[1]), jnp.float32)],
            name="out",
        )(position[None], attn, audio_out_weight)
        return video_attn, audio_out
    attn = whole_rows(position, send, keep, size)
    audio_out = lax.psum_scatter(
        jnp.dot(attn, audio_out_weight, preferred_element_type=jnp.float32),
        "head",
        scatter_dimension=0,
        tiled=True,
    )
    return video_attn, audio_out.astype(jnp.bfloat16)


def solution(mesh):
    return jax.shard_map(
        shards,
        mesh=mesh,
        in_specs=(
            P("seq", "head"),
            P(None, "seq", "head"),
            P("seq"),
            P(),
            P("seq", None, "head"),
            P(),
            P("head", "seq"),
        ),
        out_specs=(P("seq", "head"), P("head", "seq")),
        check_vma=False,
    )
```

time: 718 us -> 247 us (0.34)
  blocking collectives: 202 us -> 19.7 us
  local copies, waits for them, and re-layouts: 184 us -> 7.59 us
  matrix products: 152 us -> 0 us
  Pallas kernels: 0 us -> 111 us
  other arithmetic: 107 us -> 7.25 us
  waiting for transfers between devices: 54.1 us -> 80.6 us
  starting transfers between devices: 0.08 us -> 20 us
  between operations: 14.2 us -> 0.74 us
    dot_general x18 -> x0, matrix products: 152 us -> none  [the longest x4 40 us: audio_block(): jnp.einsum('ahd,bhd->ahb', audio_q, key, preferred_element_type=jnp.float32)]
    psum x1 -> x0, blocking collectives: 123 us -> none  [shards(): lax.psum(lax.dynamic_update_slice_in_dim(padded, partial_sum, quarter * c...]
    pallas_call x0 -> x10, Pallas kernels: none -> 111 us  [the longest x1 50.1 us: video_attend(): pl.pallas_call(functools.partial(video_kernel, pairs=pairs, block=block),...]
    ppermute x0 -> x15, waiting for transfers between devices: none -> 80.6 us  [swap(): return lax.ppermute(array, 'seq', [(i, i ^ bit) for i in range(size)])]
    sub x4 -> x0, other arithmetic: 70.8 us -> none  [video_block(): expo = jnp.exp(scores - top)]
    unnamed x3 -> x0, waiting for transfers between devices: 54.1 us -> none
    another operation x2 -> x0, local copies, waits for them, and re-layouts: 48.9 us -> none  [the longest x1 24.4 us: shards(): key_blocks = video_kv[0].reshape(blocks, block, heads, HD)]
    unnamed x1 -> x0, blocking collectives: 41.4 us -> none
  transfers between devices with their start and end apart: 2 -> 15, of which waited for: 1 -> 14; matrix products, arithmetic and copies ran while one was open for 29% -> 1% of each run, Pallas kernels for 0% -> 20%
where the time goes in v1:
time: 247 us
  Pallas kernels  111 us (45%)
  waiting for transfers between devices  80.6 us (33%)
  starting transfers between devices  20 us (8%)
  blocking collectives  19.7 us (8%)
  local copies, waits for them, and re-layouts  7.59 us (3%)
  other arithmetic  7.25 us (3%)
    ppermute x15, waiting for transfers between devices, swap(): return lax.ppermute(array, 'seq', [(i, i ^ bit) for i in range(size)])  80.6 us
    pallas_call x1, Pallas kernels, video_attend(): pl.pallas_call(functools.partial(video_kernel, pairs=pairs, block=block),...  50.1 us
    pallas_call x1, Pallas kernels, audio_partials(): pl.pallas_call(functools.partial(audio_kernel, pairs=pairs), grid_spec=pl...  40.2 us
    ppermute x15, starting transfers between devices, swap(): return lax.ppermute(array, 'seq', [(i, i ^ bit) for i in range(size)])  20 us
    all_to_all x1, blocking collectives, projected_parts(): own = lax.all_to_all(picked, 'seq', 0, 0, axis_index_groups=groups)  19.7 us
    pallas_call x4, Pallas kernels, finished_rows(): pl.pallas_call(merge_kernel, in_specs=[SMEM] + [pl.BlockSpec(memory_space...  10.6 us
    unnamed x16, local copies, waits for them, and re-layouts  6.72 us
  transfers between devices with their start and end apart: 15, of which 14 were waited for; matrix products, arithmetic and copies ran while one was open for 1% of the time, Pallas kernels for 20%

profile of v1, /device:TPU:0, one launch (start us, length us, event | category | flops | bytes accessed | tf_op | source)
XLA Modules:
  0.0 246.8 jit_solution(6833115098376876641)
XLA Ops:
  0.6 2.3 pick.1
  2.9 19.7 %all_to_all.5.weight_ref = bf16[16,192,128]{2,1,0:T(8,128)(2,1)} all-to-all(bf16[16,192,128]{2,1,0:T(8,128)(2,1)} %pick.1), channel_id=1, replica_groups={{0,1,2,3,4,5,6,7,8,9,10,11,12,13,14,15},{16,17,18,19,20,21,22,23,24,25,..., dimensions={0} | all-to-all | bytes 1572864 | tf_op jit(solution)/shard_map/all_to_all | solution.py:273
  22.7 2.7 %project.1 = bf16[192,256]{1,0:T(8,128)(2,1)} custom-call(bf16[16,192,128]{2,1,0:T(8,128)(2,1)} %all_to_all.5.weight_ref, bf16[256,2048]{1,0:T(8,128)(2,1)} %hidden_ref.1), custom_call_target="tpu_custom_call" | custom-call | tf_op jit(solution)/shard_map/project/pallas_call | solution.py:274
  25.3 2.6 %collective-permute-start = (bf16[192,256]{1,0:T(8,128)(2,1)}, bf16[192,256]{1,0:T(8,128)(2,1)S(1)}, u32[]{:S(2)}, u32[]{:S(2)}) collective-permute-start(bf16[192,256]{1,0:T(8,128)(2,1)} %project.1), channel_id=1, source_target_pairs={{0,16},{1,17},{2,18},{3,19},{4,20},{5,21},{6,22},{7,23},{8,24},{9,... | collective-permute-start | bytes 294920 | tf_op jit(solution)/shard_map/ppermute | solution.py:250
  27.9 4.6 %collective-permute-done = bf16[192,256]{1,0:T(8,128)(2,1)S(1)} collective-permute-done((bf16[192,256]{1,0:T(8,128)(2,1)}, bf16[192,256]{1,0:T(8,128)(2,1)S(1)}, u32[]{:S(2)}, u32[]{:S(2)}) %collective-permute-start) | collective-permute-done | bytes 98336 | tf_op jit(solution)/shard_map/ppermute | solution.py:250
  32.5 0.9 fusion.13
  33.9 5.9 %collective-permute-done.1 = bf16[2,192,256]{2,1,0:T(8,128)(2,1)S(1)} collective-permute-done((bf16[2,192,256]{2,1,0:T(8,128)(2,1)S(1)}, bf16[2,192,256]{2,1,0:T(8,128)(2,1)S(1)}, u32[]{:S(2)}, u32[]{:S(2)}) %collective-permute-start.1) | collective-permute-done | bytes 196640 | tf_op jit(solution)/shard_map/ppermute | solution.py:250
  39.8 1.2 collective-permute-start.2
  41.0 8.4 %collective-permute-done.2 = bf16[2,2,192,256]{3,2,1,0:T(8,128)(2,1)S(1)} collective-permute-done((bf16[2,2,192,256]{3,2,1,0:T(8,128)(2,1)S(1)}, bf16[2,2,192,256]{3,2,1,0:T(8,128)(2,1)S(1)}, u32[]{:S(2)}, u32[]{:S(2)}) %collective-permute-start.2) | collective-permute-done | bytes 393248 | tf_op jit(solution)/shard_map/ppermute | solution.py:250
  49.6 1.7 collective-permute-start.3
  51.3 15.9 %collective-permute-done.3 = bf16[2,2,2,192,256]{4,3,2,1,0:T(8,128)(2,1)S(1)} collective-permute-done((bf16[2,2,2,192,256]{4,3,2,1,0:T(8,128)(2,1)S(1)}, bf16[2,2,2,192,256]{4,3,2,1,0:T(8,128)(2,1)S(1)}, u32[]{:S(2)}, u32[]{:S(2)}) %collective-permute-start.3) | collective-permute-done | bytes 786464 | tf_op jit(solution)/shard_map/ppermute | solution.py:250
  67.9 0.8 copy.11.audio_clip_ref
  69.4 1.6 collective-permute-done.4
  71.0 3.3 %pad_maximum_fusion = bf16[2,2,2,2,2,192,256]{6,5,4,3,2,1,0:T(8,128)(2,1)} fusion(bf16[1,2,2,2,2,192,256]{6,5,4,3,2,1,0:T(8,128)(2,1)} %bitcast.14, bf16[1,2,2,2,2,192,256]{6,5,4,3,2,1,0:T(8,128)(2,1)S(1)} %get-tuple-element.26), kind=kLoop, calls=%fused_computation | loop fusion | flops 1572864 | bytes 6291456 | tf_op jit(solution)/shard_map/concatenate | solution.py:257
  74.4 40.2 %audio_partials.1 = (f32[128,2176]{1,0:T(8,128)}, f32[128,2176]{1,0:T(8,128)}) custom-call(s32[65]{0:T(128)} %pad_add_fusion.table_ref, s32[1,2048]{1,0:T(1,128)} %bitcast.55, s32[256,1]{1,0:T(8,128)} %copy.11.audio_clip_ref, bf16[6144,256]{1,0:T(8,128)(2,1)} %bitcast.40, bf16[2,2048,2048]{2,1,0:T(8,128)(2,1)} %value_ref.1, bf16[2,2048,2048]{2,1,0:T(8,128)(2,1)} %value_ref.1), custom_call_target="tpu_custom_call" | custom-call | tf_op jit(solution)/shard_map/audio_partials/pallas_call | solution.py:102
  114.7 2.8 %collective-permute-done.5.other_ref = f32[128,2176]{1,0:T(8,128)S(1)} collective-permute-done((f32[128,2176]{1,0:T(8,128)}, f32[128,2176]{1,0:T(8,128)S(1)}, u32[]{:S(2)}, u32[]{:S(2)}) %collective-permute-start.5) | collective-permute-done | bytes 1114144 | tf_op jit(solution)/shard_map/ppermute | solution.py:250
  117.5 1.0 copy-done
  118.5 3.8 %merge.4 = (f32[64,2176]{1,0:T(8,128)}, f32[64,2176]{1,0:T(8,128)}) custom-call(s32[1]{0:T(128)} %bitcast.20.bit_ref, f32[128,2176]{1,0:T(8,128)} %get-tuple-element.12.keep_ref, f32[128,2176]{1,0:T(8,128)} %copy-done), custom_call_target="tpu_custom_call" | custom-call | tf_op jit(solution)/shard_map/merge/pallas_call | solution.py:306
  122.3 1.7 collective-permute-start.6
  124.0 13.1 %collective-permute-done.6.other_ref = f32[64,2176]{1,0:T(8,128)S(1)} collective-permute-done((f32[64,2176]{1,0:T(8,128)}, f32[64,2176]{1,0:T(8,128)S(1)}, u32[]{:S(2)}, u32[]{:S(2)}) %collective-permute-start.6) | collective-permute-done | bytes 557088 | tf_op jit(solution)/shard_map/ppermute | solution.py:250
  137.2 0.8 copy-done.1
  138.0 2.8 %merge.5 = (f32[32,2176]{1,0:T(8,128)}, f32[32,2176]{1,0:T(8,128)}) custom-call(s32[1]{0:T(128)} %bitcast.19.bit_ref, f32[64,2176]{1,0:T(8,128)} %get-tuple-element.14.keep_ref, f32[64,2176]{1,0:T(8,128)} %copy-done.1), custom_call_target="tpu_custom_call" | custom-call | tf_op jit(solution)/shard_map/merge/pallas_call | solution.py:306
  140.7 1.6 collective-permute-start.7
  142.3 6.5 %collective-permute-done.7.other_ref = f32[32,2176]{1,0:T(8,128)S(1)} collective-permute-done((f32[32,2176]{1,0:T(8,128)}, f32[32,2176]{1,0:T(8,128)S(1)}, u32[]{:S(2)}, u32[]{:S(2)}) %collective-permute-start.7) | collective-permute-done | bytes 278560 | tf_op jit(solution)/shard_map/ppermute | solution.py:250
  148.8 0.7 copy-done.2
  149.5 2.2 merge.6
  151.7 0.7 collective-permute-start.8
  152.4 4.6 %collective-permute-done.8.other_ref = f32[16,2176]{1,0:T(8,128)S(1)} collective-permute-done((f32[16,2176]{1,0:T(8,128)}, f32[16,2176]{1,0:T(8,128)S(1)}, u32[]{:S(2)}, u32[]{:S(2)}) %collective-permute-start.8) | collective-permute-done | bytes 139296 | tf_op jit(solution)/shard_map/ppermute | solution.py:250
  157.0 0.7 copy-done.4
  157.6 1.9 merge.7
  159.5 2.6 %collective-permute-start.9 = (f32[8,2176]{1,0:T(8,128)}, f32[8,2176]{1,0:T(8,128)S(1)}, u32[]{:S(2)}, u32[]{:S(2)}) collective-permute-start(f32[8,2176]{1,0:T(8,128)} %get-tuple-element.21), channel_id=1, source_target_pairs={{0,16},{1,17},{2,18},{3,19},{4,20},{5,21},{6,22},{7,23},{8,24},{9,... | collective-permute-start | bytes 208904 | tf_op jit(solution)/shard_map/ppermute | solution.py:250
  162.2 3.5 %collective-permute-done.9.other_ref = f32[8,2176]{1,0:T(8,128)S(1)} collective-permute-done((f32[8,2176]{1,0:T(8,128)}, f32[8,2176]{1,0:T(8,128)S(1)}, u32[]{:S(2)}, u32[]{:S(2)}) %collective-permute-start.9) | collective-permute-done | bytes 69664 | tf_op jit(solution)/shard_map/ppermute | solution.py:250
  165.7 0.6 copy-done.5
  166.3 1.8 finish.1
  168.1 2.0 collective-permute-start.10
  170.1 3.0 %collective-permute-done.10 = bf16[8,2048]{1,0:T(8,128)(2,1)S(1)} collective-permute-done((bf16[8,2048]{1,0:T(8,128)(2,1)}, bf16[8,2048]{1,0:T(8,128)(2,1)S(1)}, u32[]{:S(2)}, u32[]{:S(2)}) %collective-permute-start.10) | collective-permute-done | bytes 32800 | tf_op jit(solution)/shard_map/ppermute | solution.py:250
  173.1 0.8 fusion.11
  173.9 1.3 collective-permute-start.11
  175.2 3.0 %collective-permute-done.11 = bf16[2,8,2048]{2,1,0:T(8,128)(2,1)S(1)} collective-permute-done((bf16[2,8,2048]{2,1,0:T(8,128)(2,1)S(1)}, bf16[2,8,2048]{2,1,0:T(8,128)(2,1)S(1)}, u32[]{:S(2)}, u32[]{:S(2)}) %collective-permute-start.11) | collective-permute-done | bytes 65568 | tf_op jit(solution)/shard_map/ppermute | solution.py:250
  178.3 1.8 collective-permute-start.12
  180.1 3.2 %collective-permute-done.12 = bf16[2,2,8,2048]{3,2,1,0:T(8,128)(2,1)S(1)} collective-permute-done((bf16[2,2,8,2048]{3,2,1,0:T(8,128)(2,1)S(1)}, bf16[2,2,8,2048]{3,2,1,0:T(8,128)(2,1)S(1)}, u32[]{:S(2)}, u32[]{:S(2)}) %collective-permute-start.12) | collective-permute-done | bytes 131104 | tf_op jit(solution)/shard_map/ppermute | solution.py:250
  183.3 2.0 collective-permute-start.13
  185.3 4.5 %collective-permute-done.13 = bf16[2,2,2,8,2048]{4,3,2,1,0:T(8,128)(2,1)S(1)} collective-permute-done((bf16[2,2,2,8,2048]{4,3,2,1,0:T(8,128)(2,1)S(1)}, bf16[2,2,2,8,2048]{4,3,2,1,0:T(8,128)(2,1)S(1)}, u32[]{:S(2)}, u32[]{:S(2)}) %collective-permute-start.13) | collective-permute-done | bytes 262176 | tf_op jit(solution)/shard_map/ppermute | solution.py:250
  189.9 1.0 copy.13.weight_ref
  190.9 50.1 %video_attend.1 = bf16[2048,2048]{1,0:T(8,128)(2,1)} custom-call(s32[65]{0:T(128)} %pad_add_fusion.table_ref, s32[1,2048]{1,0:T(1,128)} %bitcast.56, s32[256,1]{1,0:T(8,128)} %copy.11.audio_clip_ref, bf16[6144,256]{1,0:T(8,128)(2,1)} %bitcast.41, bf16[2048,2048]{1,0:T(8,128)(2,1)} %query_ref.1), custom_call_target="tpu_custom_call" | custom-call | tf_op jit(solution)/shard_map/video_attend/pallas_call | solution.py:165
  241.1 1.1 pad_maximum_fusion.2
  242.2 3.1 %out.1 = bf16[256,64]{1,0:T(8,128)(2,1)} custom-call(s32[1]{0:T(128)} %bitcast.16.position_ref, bf16[256,2048]{1,0:T(8,128)(2,1)} %bitcast.42, bf16[2048,64]{1,0:T(8,128)(2,1)} %copy.13.weight_ref), custom_call_target="tpu_custom_call" | custom-call | tf_op jit(solution)/shard_map/out/pallas_call | solution.py:354
  245.2 1.5 copy.14
  (24 shorter events, 2.4 us)
Async XLA Ops:
  25.3 7.2 %collective-permute-start = (bf16[192,256]{1,0:T(8,128)(2,1)}, bf16[192,256]{1,0:T(8,128)(2,1)S(1)}, u32[]{:S(2)}, u32[]{:S(2)}) collective-permute-start(bf16[192,256]{1,0:T(8,128)(2,1)} %project.1), channel_id=1, source_target_pairs={{0,16},{1,17},{2,18},{3,19},{4,20},{5,21},{6,22},{7,23},{8,24},{9,... | collective-permute-start | bytes 294920 | tf_op jit(solution)/shard_map/ppermute | solution.py:250
  33.4 6.3 %collective-permute-start.1 = (bf16[2,192,256]{2,1,0:T(8,128)(2,1)S(1)}, bf16[2,192,256]{2,1,0:T(8,128)(2,1)S(1)}, u32[]{:S(2)}, u32[]{:S(2)}) collective-permute-start(bf16[2,192,256]{2,1,0:T(8,128)(2,1)S(1)} %get-tuple-element.37), channel_id=1, source_target_pairs={{0,8},{1,9},{2,10},{3,11},{4,12},{5,13},{6,14},{7,15},{8,0},{9,1},... | collective-permute-start | bytes 589832 | tf_op jit(solution)/shard_map/ppermute | solution.py:250
  39.8 9.7 %collective-permute-start.2 = (bf16[2,2,192,256]{3,2,1,0:T(8,128)(2,1)S(1)}, bf16[2,2,192,256]{3,2,1,0:T(8,128)(2,1)S(1)}, u32[]{:S(2)}, u32[]{:S(2)}) collective-permute-start(bf16[2,2,192,256]{3,2,1,0:T(8,128)(2,1)S(1)} %get-tuple-element.33), channel_id=1, source_target_pairs={{0,4},{1,5},{2,6},{3,7},{4,0},{5,1},{6,2},{7,3},{8,12},{9,13},{10,... | collective-permute-start | bytes 1179656 | tf_op jit(solution)/shard_map/ppermute | solution.py:250
  49.6 17.6 %collective-permute-start.3 = (bf16[2,2,2,192,256]{4,3,2,1,0:T(8,128)(2,1)S(1)}, bf16[2,2,2,192,256]{4,3,2,1,0:T(8,128)(2,1)S(1)}, u32[]{:S(2)}, u32[]{:S(2)}) collective-permute-start(bf16[2,2,2,192,256]{4,3,2,1,0:T(8,128)(2,1)S(1)} %get-tuple-element.29), channel_id=1, source_target_pairs={{0,2},{1,3},{2,0},{3,1},{4,6},{5,7},{6,4},{7,5},{8,10},{9,11},{10,... | collective-permute-start | bytes 2359304 | tf_op jit(solution)/shard_map/ppermute | solution.py:250
  67.2 0.7 copy-start.6
  67.4 3.6 %collective-permute-start.4 = (bf16[2,2,2,2,192,256]{5,4,3,2,1,0:T(8,128)(2,1)S(1)}, bf16[2,2,2,2,192,256]{5,4,3,2,1,0:T(8,128)(2,1)}, u32[]{:S(2)}, u32[]{:S(2)}) collective-permute-start(bf16[2,2,2,2,192,256]{5,4,3,2,1,0:T(8,128)(2,1)S(1)} %get-tuple-element.27), channel_id=1, source_target_pairs={{0,1},{1,0},{2,3},{3,2},{4,5},{5,4},{6,7},{7,6},{8,9},{9,8},{10,11... | collective-permute-start | bytes 4718600 | tf_op jit(solution)/shard_map/ppermute | solution.py:250
  114.5 3.0 %collective-permute-start.5 = (f32[128,2176]{1,0:T(8,128)}, f32[128,2176]{1,0:T(8,128)S(1)}, u32[]{:S(2)}, u32[]{:S(2)}) collective-permute-start(f32[128,2176]{1,0:T(8,128)} %get-tuple-element.13), channel_id=1, source_target_pairs={{0,1},{1,0},{2,3},{3,2},{4,5},{5,4},{6,7},{7,6},{8,9},{9,8},{10,11... | collective-permute-start | bytes 3342344 | tf_op jit(solution)/shard_map/ppermute | solution.py:250
  117.5 1.0 copy-start
  122.3 14.9 %collective-permute-start.6 = (f32[64,2176]{1,0:T(8,128)}, f32[64,2176]{1,0:T(8,128)S(1)}, u32[]{:S(2)}, u32[]{:S(2)}) collective-permute-start(f32[64,2176]{1,0:T(8,128)} %get-tuple-element.15), channel_id=1, source_target_pairs={{0,2},{1,3},{2,0},{3,1},{4,6},{5,7},{6,4},{7,5},{8,10},{9,11},{10,... | collective-permute-start | bytes 1671176 | tf_op jit(solution)/shard_map/ppermute | solution.py:250
  137.2 0.8 copy-start.1
  140.7 8.1 %collective-permute-start.7 = (f32[32,2176]{1,0:T(8,128)}, f32[32,2176]{1,0:T(8,128)S(1)}, u32[]{:S(2)}, u32[]{:S(2)}) collective-permute-start(f32[32,2176]{1,0:T(8,128)} %get-tuple-element.17), channel_id=1, source_target_pairs={{0,4},{1,5},{2,6},{3,7},{4,0},{5,1},{6,2},{7,3},{8,12},{9,13},{10,... | collective-permute-start | bytes 835592 | tf_op jit(solution)/shard_map/ppermute | solution.py:250
  148.8 0.7 copy-start.2
  151.7 5.3 %collective-permute-start.8 = (f32[16,2176]{1,0:T(8,128)}, f32[16,2176]{1,0:T(8,128)S(1)}, u32[]{:S(2)}, u32[]{:S(2)}) collective-permute-start(f32[16,2176]{1,0:T(8,128)} %get-tuple-element.19), channel_id=1, source_target_pairs={{0,8},{1,9},{2,10},{3,11},{4,12},{5,13},{6,14},{7,15},{8,0},{9,1},... | collective-permute-start | bytes 417800 | tf_op jit(solution)/shard_map/ppermute | solution.py:250
  157.0 0.7 copy-start.4
  159.5 30.4 %copy-start.3 = (bf16[2048,64]{0,1:T(8,128)(2,1)S(1)}, bf16[2048,64]{0,1:T(8,128)(2,1)}, u32[]{:S(2)}) copy-start(bf16[2048,64]{0,1:T(8,128)(2,1)} %param.13) | copy-start | bytes 786436
  159.5 6.2 %collective-permute-start.9 = (f32[8,2176]{1,0:T(8,128)}, f32[8,2176]{1,0:T(8,128)S(1)}, u32[]{:S(2)}, u32[]{:S(2)}) collective-permute-start(f32[8,2176]{1,0:T(8,128)} %get-tuple-element.21), channel_id=1, source_target_pairs={{0,16},{1,17},{2,18},{3,19},{4,20},{5,21},{6,22},{7,23},{8,24},{9,... | collective-permute-start | bytes 208904 | tf_op jit(solution)/shard_map/ppermute | solution.py:250
  165.7 0.6 copy-start.5
  168.1 5.0 %collective-permute-start.10 = (bf16[8,2048]{1,0:T(8,128)(2,1)}, bf16[8,2048]{1,0:T(8,128)(2,1)S(1)}, u32[]{:S(2)}, u32[]{:S(2)}) collective-permute-start(bf16[8,2048]{1,0:T(8,128)(2,1)} %finish.1), channel_id=1, source_target_pairs={{0,16},{1,17},{2,18},{3,19},{4,20},{5,21},{6,22},{7,23},{8,24},{9,... | collective-permute-start | bytes 98312 | tf_op jit(solution)/shard_map/ppermute | solution.py:250
  173.9 4.3 %collective-permute-start.11 = (bf16[2,8,2048]{2,1,0:T(8,128)(2,1)S(1)}, bf16[2,8,2048]{2,1,0:T(8,128)(2,1)S(1)}, u32[]{:S(2)}, u32[]{:S(2)}) collective-permute-start(bf16[2,8,2048]{2,1,0:T(8,128)(2,1)S(1)} %get-tuple-element.41), channel_id=1, source_target_pairs={{0,8},{1,9},{2,10},{3,11},{4,12},{5,13},{6,14},{7,15},{8,0},{9,1},... | collective-permute-start | bytes 196616 | tf_op jit(solution)/shard_map/ppermute | solution.py:250
  178.3 5.0 %collective-permute-start.12 = (bf16[2,2,8,2048]{3,2,1,0:T(8,128)(2,1)S(1)}, bf16[2,2,8,2048]{3,2,1,0:T(8,128)(2,1)S(1)}, u32[]{:S(2)}, u32[]{:S(2)}) collective-permute-start(bf16[2,2,8,2048]{3,2,1,0:T(8,128)(2,1)S(1)} %get-tuple-element.39), channel_id=1, source_target_pairs={{0,4},{1,5},{2,6},{3,7},{4,0},{5,1},{6,2},{7,3},{8,12},{9,13},{10,... | collective-permute-start | bytes 393224 | tf_op jit(solution)/shard_map/ppermute | solution.py:250
  183.3 6.4 %collective-permute-start.13 = (bf16[2,2,2,8,2048]{4,3,2,1,0:T(8,128)(2,1)S(1)}, bf16[2,2,2,8,2048]{4,3,2,1,0:T(8,128)(2,1)S(1)}, u32[]{:S(2)}, u32[]{:S(2)}) collective-permute-start(bf16[2,2,2,8,2048]{4,3,2,1,0:T(8,128)(2,1)S(1)} %get-tuple-element.35), channel_id=1, source_target_pairs={{0,2},{1,3},{2,0},{3,1},{4,6},{5,7},{6,4},{7,5},{8,10},{9,11},{10,... | collective-permute-start | bytes 786440 | tf_op jit(solution)/shard_map/ppermute | solution.py:250
  189.8 51.2 %collective-permute-start.14 = (bf16[2,2,2,2,8,2048]{5,4,3,2,1,0:T(8,128)(2,1)S(1)}, bf16[2,2,2,2,8,2048]{5,4,3,2,1,0:T(8,128)(2,1)S(1)}, u32[]{:S(2)}, u32[]{:S(2)}) collective-permute-start(bf16[2,2,2,2,8,2048]{5,4,3,2,1,0:T(8,128)(2,1)S(1)} %get-tuple-element.31), channel_id=1, source_target_pairs={{0,1},{1,0},{2,3},{3,2},{4,5},{5,4},{6,7},{7,6},{8,9},{9,8},{10,11... | collective-permute-start | bytes 1572872 | tf_op jit(solution)/shard_map/ppermute | solution.py:250
